TPU v7x, 32 devices: a whole 2x2x4 slice. The times are simulated.
32 devices in a mesh: groups: 2 (over x), dp: 16 (over z, y, core).
Axes of the slice: x: 2, y: 2, z: 4, core: 2. Of those that a mesh axis runs over, the one named last changes fastest.
Arguments:
- states: bfloat16 [16384, 1024], P(('groups', 'dp')), parts along dimension 0, may hold values from -6 to 6
- lengths: int32 [64], P(('groups', 'dp')), parts along dimension 0, may hold values from 1 to 256, as said below
- norm_gain: bfloat16 [1024], replicated, may hold values from 0.5 to 2
- w_gate: bfloat16 [1024, 1536], replicated, may hold values from -0.1875 to 0.1875
- w_up: bfloat16 [1024, 1536], replicated, may hold values from -0.1875 to 0.1875
- w_down: bfloat16 [1536, 1024], replicated, may hold values from -0.15625 to 0.15625
- context: bfloat16 [64, 4096], P('groups', 'dp'), parts along dimension 0, may hold values from -6 to 6
- w_out: bfloat16 [4096, 4096], P('dp'), may hold values from -0.09375 to 0.09375
- resid_stream: bfloat16 [64, 4096], P('groups'), parts along dimension 0, may hold values from -6 to 6
- teacher_gain: bfloat16 [4096], replicated, may hold values from 0.5 to 2
Outputs:
- gram_loss: float32 [2], P('groups'), parts along dimension 0
- grad_gate: float32 [2048, 1536], P(('groups', 'dp')), parts along dimension 0
- grad_up: float32 [2048, 1536], P(('groups', 'dp')), parts along dimension 0
- grad_down: float32 [3072, 1024], P(('groups', 'dp')), parts along dimension 0
There are 2 independent parts, one for each index of `groups`. A program takes and returns all parts, laid end to end along the dimension named above; an argument that names none is the same for every part. Nothing has to cross between parts.
Inputs may be any that keep to these rules, and one draw needn't show every extreme that they name: `lengths`: some document of every group fills all 256 slots and some has a single valid token.
All inputs are finite; a program needn't handle non-finite values.
Results may differ from a plain program's by a relative error of at most 0.004.
Values may be sent and summed in bfloat16 or wider, within the bound.
A program may use at most 128 MiB of HBM per device.

v0:
```python
import jax
import jax.numpy as jnp
from jax import lax
from jax.sharding import PartitionSpec as P

EPS = 1e-06
LOSS_SCALE = 4096.0


def teacher_embed(attn_rows, resid_rows, teacher_gain):
    scaled_rows = teacher_gain.astype(jnp.float32) * (resid_rows.astype(jnp.float32) + attn_rows)
    inv_teacher = lax.rsqrt(jnp.sum(scaled_rows * scaled_rows, axis=1, keepdims=True) + EPS)
    return (scaled_rows * inv_teacher).astype(jnp.bfloat16)


def rows_product(left_rows, right_rows):
    return lax.dot_general(
        left_rows, right_rows, (((1,), (1,)), ((), ())), preferred_element_type=jnp.float32
    )


def cols_product(left_cols, right_cols):
    return lax.dot_general(
        left_cols, right_cols, (((0,), (0,)), ((), ())), preferred_element_type=jnp.float32
    )


def per_device(
    states, lengths, norm_gain, w_gate, w_up, w_down, context, w_out, resid_stream, teacher_gain
):
    dp = lax.axis_size("dp")
    my_index = lax.axis_index("dp")
    doc_dev = lengths.shape[0]
    seq_len = states.shape[0] // doc_dev
    model_width = states.shape[1]
    hidden_width = w_gate.shape[1]
    feat = w_out.shape[1] // dp
    high = lax.Precision.HIGHEST
    partial_attn = jnp.dot(context, w_out, preferred_element_type=jnp.float32)
    attn_cols = lax.psum_scatter(partial_attn, "dp", scatter_dimension=1, tiled=True)
    resid_cols = lax.dynamic_slice_in_dim(resid_stream, my_index * feat, feat, 1)
    gain_cols = lax.dynamic_slice_in_dim(teacher_gain, my_index * feat, feat, 0)
    scaled = gain_cols.astype(jnp.float32) * (resid_cols.astype(jnp.float32) + attn_cols)
    gram_part = lax.dot_general(scaled, scaled, (((1,), (1,)), ((), ())), precision=high)
    states_wide = states.astype(jnp.float32)
    inv_rms = lax.rsqrt(jnp.mean(states_wide * states_wide, axis=1, keepdims=True) + EPS)
    normed = (states_wide * inv_rms * norm_gain.astype(jnp.float32)).astype(jnp.bfloat16)
    gate_pre = jnp.dot(normed, w_gate, preferred_element_type=jnp.float32)
    up_pre = jnp.dot(normed, w_up, preferred_element_type=jnp.float32)
    hidden = (jax.nn.silu(gate_pre) * up_pre).astype(jnp.bfloat16)
    positions = lax.broadcasted_iota(jnp.int32, (doc_dev, seq_len), 1)
    valid_mask = (positions < lengths[:, None]).astype(jnp.float32)
    counts = lengths.astype(jnp.float32)
    hidden_sum = jnp.sum(
        hidden.astype(jnp.float32).reshape(doc_dev, seq_len, hidden_width) * valid_mask[:, :, None],
        axis=1,
    )
    state_sum = jnp.sum(
        states_wide.reshape(doc_dev, seq_len, model_width) * valid_mask[:, :, None], axis=1
    )
    packed = jnp.concatenate(
        [hidden_sum, state_sum, jnp.broadcast_to(counts[:, None], (doc_dev, 128))], axis=1
    )
    packed_all = lax.all_gather(packed, "dp", axis=0, tiled=True)
    hidden_all = packed_all[:, :hidden_width]
    state_all = packed_all[:, hidden_width : hidden_width + model_width]
    count_all = packed_all[:, hidden_width + model_width :][:, :1]
    gram_raw = lax.psum(gram_part, "dp")
    docs = gram_raw.shape[0]
    eye = jnp.eye(docs, dtype=jnp.float32)
    inv_col = lax.rsqrt(jnp.sum(gram_raw * eye, axis=1, keepdims=True) + EPS)
    inv_row = lax.rsqrt(jnp.sum(gram_raw * eye, axis=0, keepdims=True) + EPS)
    gram_teacher = gram_raw * inv_col * inv_row
    pooled = (
        state_all + jnp.dot(hidden_all, w_down.astype(jnp.float32), precision=high)
    ) / count_all
    inv_norm = lax.rsqrt(jnp.sum(pooled * pooled, axis=1, keepdims=True) + EPS)
    unit_rows = pooled * inv_norm
    embed = unit_rows.astype(jnp.bfloat16)
    gram_diff = rows_product(embed, embed) - gram_teacher
    diff_norm = jnp.sqrt(jnp.sum(gram_diff * gram_diff) + EPS)
    teacher_norm = jnp.sqrt(jnp.sum(gram_teacher * gram_teacher))
    gram_loss = (diff_norm / teacher_norm).reshape(1)
    d_gram = LOSS_SCALE * gram_diff / (diff_norm * teacher_norm)
    d_embed = 2.0 * jnp.dot(d_gram, embed.astype(jnp.float32), precision=high)
    along = jnp.sum(unit_rows * d_embed, axis=1, keepdims=True)
    d_pooled = (d_embed - unit_rows * along) * inv_norm
    d_all = (d_pooled / count_all).astype(jnp.bfloat16)
    down_rows = hidden_width // dp
    own_hidden = lax.dynamic_slice_in_dim(hidden_all, my_index * down_rows, down_rows, 1)
    grad_down = lax.dot_general(
        own_hidden, d_all.astype(jnp.float32), (((0,), (0,)), ((), ())), precision=high
    )
    d_doc = lax.dynamic_slice_in_dim(d_all, my_index * doc_dev, doc_dev, 0)
    d_hidden = rows_product(d_doc, w_down)
    d_hidden_tok = (d_hidden[:, None, :] * valid_mask[:, :, None]).reshape(
        doc_dev * seq_len, hidden_width
    )
    sigmoid_gate = jax.nn.sigmoid(gate_pre)
    d_gate = (
        d_hidden_tok * up_pre * sigmoid_gate * (1.0 + gate_pre * (1.0 - sigmoid_gate))
    ).astype(jnp.bfloat16)
    d_up = (d_hidden_tok * jax.nn.silu(gate_pre)).astype(jnp.bfloat16)
    rows = model_width // dp
    terms = jnp.concatenate([cols_product(normed, d_gate), cols_product(normed, d_up)], axis=1)
    terms = terms.astype(jnp.bfloat16)
    swapped = lax.all_to_all(terms.reshape(dp, rows, 2 * hidden_width), "dp", 0, 0)
    total = jnp.sum(swapped.astype(jnp.float32), axis=0)
    return (gram_loss, total[:, :hidden_width], total[:, hidden_width:], grad_down)


def solution(mesh):
    in_specs = (
        P(("groups", "dp"), None),
        P(("groups", "dp")),
        P(),
        P(),
        P(),
        P(),
        P("groups", "dp"),
        P("dp", None),
        P("groups", None),
        P(),
    )
    out_specs = (
        P("groups"),
        P(("groups", "dp"), None),
        P(("groups", "dp"), None),
        P(("groups", "dp"), None),
    )
    return jax.shard_map(
        per_device, mesh=mesh, in_specs=in_specs, out_specs=out_specs, check_vma=False
    )
```

profile of v0, /device:TPU:13, one launch (start us, length us, event | category | flops | bytes accessed | tf_op | source)
XLA Modules:
  0.0 300.5 jit_solution(8370609172329494020)
XLA Ops:
  7.2 0.0 copy-start
  7.2 0.0 copy-start.7
  7.2 0.0 copy-start.6
  7.2 0.0 reduce-scatter.2.cloned.1.call-start
  7.2 3.0 %fusion.35 = f32[32,4096]{1,0:T(8,128)} fusion(bf16[32,256]{1,0:T(8,128)(2,1)} %param.16, bf16[256,4096]{1,0:T(8,128)(2,1)} %param.17), kind=kOutput, calls=%fused_computation.65 | convolution fusion | flops 67108864 | bytes 2637824 | tf_op jit(solution)/shard_map/dot_general | solution.py:39
  10.3 0.0 reduce-scatter.2.cloned.1.call-update
  10.3 0.0 copy-done.7
  10.3 0.1 fusion.30
  10.4 1.5 multiply_reduce_fusion.1
  11.9 0.0 copy-done.6
  11.9 1.5 multiply_reduce_fusion
  13.5 0.0 copy-start.3
  13.5 4.2 %fusion.33 = f32[512,1536]{1,0:T(8,128)S(1)} fusion(bf16[1024,1536]{1,0:T(8,128)(2,1)} %param.13, f32[1024]{0:T(1024)S(1)} %convert_element_type.57, f32[512]{0:T(512)S(1)} %add_rsqrt_fusion, bf16[512,1024]{1,0:T(8,128)(2,1)} %param.10), kind=kOutput, calls=%fused_computation.63 | convolution fusion | flops 1612709888 | bytes 7346176 | tf_op jit(solution)/shard_map/dot_general | solution.py:48
  17.7 0.0 copy-done
  17.7 0.0 copy-done.3
  17.7 0.0 copy-start.1
  17.7 3.9 %fusion = (f32[2,1536]{1,0:T(2,128)S(1)}, f32[512,1536]{1,0:T(8,128)}) fusion(f32[2,256]{1,0:T(2,128)S(1)} %get-tuple-element.11, f32[512,1536]{1,0:T(8,128)S(1)} %fusion.33, bf16[1024,1536]{1,0:T(8,128)(2,1)S(1)} %copy-done, f32[1024]{0:T(1024)S(1)} %convert_element_type.57, f32[512]{0:T(512)S(1)} %add_rsqrt_fusion, bf16[512,1024]{1,0:T(8,128)(2,1)S(1)} %copy-done.3), kind=kOutput, calls=%fused_computation.5 | convolution fusion | flops 1619784704 | bytes 10506240 | tf_op jit(solution)/shard_map/dot_general | solution.py:49
  21.6 0.0 copy-done.1
  21.6 0.1 broadcast_in_dim.2
  21.6 18.0 %all-gather = f32[16,2,2688]{2,1,0:T(2,128)} all-gather(f32[1,2,2688]{2,1,0:T(2,128)S(1)} %maximum_bitcast_fusion), channel_id=1, replica_groups=mesh['groups'=2,'dp'=16] {'dp'}, dimensions={0}, use_global_device_ids=true | all-gather | bytes 365568 | tf_op jit(solution)/shard_map/all_gather | solution.py:64
  39.6 1.2 reshape.93
  40.9 0.0 copy-start.5
  40.9 0.8 dynamic-slice_convert_fusion
  41.7 0.0 copy-done.5
  41.7 0.1 slice_reduce_fusion
  41.8 3.7 %multiply_reduce_fusion.3 = (f32[32]{0:T(128)S(1)}, f32[32,1024]{1,0:T(8,128)S(1)}) fusion(f32[32]{0:T(128)S(1)} %slice_reduce_fusion, bf16[1536,1024]{1,0:T(8,128)(2,1)} %param.15, f32[32,2688]{1,0:T(8,128)} %copy-done.5), kind=kOutput, calls=%fused_computation.25 | convolution fusion | flops 604110848 | bytes 3604736 | tf_op jit(solution)/shard_map/dot_general | solution.py:75
  45.5 20.7 %reduce-scatter.2.cloned.1.call-done = f32[32,256]{1,0:T(8,128)} async-done(((f32[32,4096]{1,0:T(8,128)}), f32[32,256]{1,0:T(8,128)}) %reduce-scatter.2.cloned.1.call-update) | async-done | bytes 32784 | tf_op jit(solution)/shard_map/reduce_scatter | solution.py:40
  66.2 1.0 fusion.9
  67.2 45.7 %psum.7 = f32[32,32]{1,0:T(8,128)S(1)} all-reduce(f32[32,32]{1,0:T(8,128)S(1)} %fusion.9), channel_id=1, replica_groups=mesh['groups'=2,'dp'=16] {'dp'}, use_global_device_ids=true, to_apply=%region_5.6 | all-reduce | flops 1024 | bytes 8192 | tf_op jit(solution)/shard_map/psum | solution.py:68
  112.9 0.1 fusion.21
  113.1 0.7 multiply_reduce_fusion.4
  114.4 0.8 multiply_reduce_fusion.5
  116.0 0.0 copy-start.2
  116.0 0.4 multiply_reduce_fusion.2
  116.3 0.1 divide_convert_fusion
  116.4 3.0 %fusion.24 = f32[2,1536]{1,0:T(2,128)S(1)} fusion(bf16[1536,1024]{1,0:T(8,128)(2,1)} %param.15, bf16[32,1024]{1,0:T(8,128)(2,1)S(1)} %divide_convert_fusion, s32[]{:T(128)S(6)} %select_n.11), kind=kOutput, calls=%fused_computation.48 | convolution fusion | flops 6291456 | bytes 3162116 | tf_op jit(solution)/shard_map/dot_general | solution.py:17
  119.5 0.0 copy-done.2
  119.5 0.0 copy-start.4
  119.5 3.5 %fusion.5 = (bf16[512,1536]{1,0:T(8,128)(2,1)S(1)}, bf16[512,1536]{1,0:T(8,128)(2,1)S(1)}) fusion(f32[512,1536]{1,0:T(8,128)} %get-tuple-element.13, f32[512,1536]{1,0:T(8,128)S(1)} %copy-done.2, f32[512]{0:T(512)S(1)} %bitcast.38, f32[2,1536]{1,0:T(2,128)S(1)} %fusion.24), kind=kLoop, calls=%fused_computation.11 | loop fusion | flops 11010048 | bytes 9451520 | tf_op jit(solution)/shard_map/convert_element_type | solution.py:102
  123.0 0.0 copy-done.4
  123.0 1.9 convolution_convert_fusion.1
  125.0 1.9 convolution_convert_fusion
  126.9 3.5 %pad_maximum_fusion = bf16[16,64,3072]{2,1,0:T(8,128)(2,1)} fusion(bf16[16,64,1536]{2,1,0:T(8,128)(2,1)S(1)} %bitcast.37, bf16[16,64,1536]{2,1,0:T(8,128)(2,1)S(1)} %bitcast.36), kind=kLoop, calls=%fused_computation.1 | loop fusion | flops 12582912 | bytes 12582912 | tf_op jit(solution)/shard_map/concatenate | solution.py:105
  130.4 0.0 slice-start
  130.4 19.8 %all-to-all-start = ((bf16[16,64,3072]{2,1,0:T(8,128)(2,1)}), bf16[16,64,3072]{2,1,0:T(8,128)(2,1)}, u32[]{:S(2)}, u32[]{:S(2)}) async-start(bf16[16,64,3072]{2,1,0:T(8,128)(2,1)} %pad_maximum_fusion), calls=%async_computation.1 | async-start | bytes 12582912 | tf_op jit(solution)/shard_map/all_to_all | solution.py:107
  150.2 0.0 slice-done
  150.2 1.2 fusion.13
  151.4 136.2 %all-to-all-done = bf16[16,64,3072]{2,1,0:T(8,128)(2,1)} async-done(((bf16[16,64,3072]{2,1,0:T(8,128)(2,1)}), bf16[16,64,3072]{2,1,0:T(8,128)(2,1)}, u32[]{:S(2)}, u32[]{:S(2)}) %all-to-all-start) | async-done | bytes 6291488 | tf_op jit(solution)/shard_map/all_to_all | solution.py:107
  287.6 4.0 %convert_reduce_fusion = f32[64,3072]{1,0:T(8,128)S(1)} fusion(bf16[16,64,3072]{2,1,0:T(8,128)(2,1)} %all-to-all-done), kind=kLoop, calls=%fused_computation | loop fusion | flops 6094848 | bytes 7077888 | tf_op jit(solution)/shard_map/reduce_sum | solution.py:108
  291.6 0.9 fusion.34
  (7 shorter events, 0.0 us)
Async XLA Ops:
  7.2 10.5 %copy-start = (bf16[1024,1536]{1,0:T(8,128)(2,1)S(1)}, bf16[1024,1536]{1,0:T(8,128)(2,1)}, u32[]{:S(2)}) copy-start(bf16[1024,1536]{1,0:T(8,128)(2,1)} %param.14) | copy-start | bytes 9437188
  7.2 3.1 %copy-start.7 = (s32[2]{0:T(128)S(1)}, s32[2]{0:T(128)}, u32[]{:S(2)}) copy-start(s32[2]{0:T(128)} %param.11) | copy-start | bytes 28
  7.2 4.7 %copy-start.6 = (bf16[1024]{0:T(1024)(128)(2,1)S(1)}, bf16[1024]{0:T(1024)(128)(2,1)}, u32[]{:S(2)}) copy-start(bf16[1024]{0:T(1024)(128)(2,1)} %param.12) | copy-start | bytes 6148
  7.2 59.0 %reduce-scatter.2.cloned.1.call-start = ((), (), s32[]{:S(2)}) async-start(), calls=%async_computation.2 | async-start | bytes 557056 | tf_op jit(solution)/shard_map/reduce_scatter | solution.py:40
  13.5 4.2 %copy-start.3 = (bf16[512,1024]{1,0:T(8,128)(2,1)S(1)}, bf16[512,1024]{1,0:T(8,128)(2,1)}, u32[]{:S(2)}) copy-start(bf16[512,1024]{1,0:T(8,128)(2,1)} %param.10) | copy-start | bytes 3145732
  17.7 3.9 %copy-start.1 = (f32[512,1536]{1,0:T(8,128)}, f32[512,1536]{1,0:T(8,128)S(1)}, u32[]{:S(2)}) copy-start(f32[512,1536]{1,0:T(8,128)S(1)} %fusion.33) | copy-start | bytes 9437188
  40.9 0.8 copy-start.5
  116.0 3.5 %copy-start.2 = (f32[512,1536]{1,0:T(8,128)S(1)}, f32[512,1536]{1,0:T(8,128)}, u32[]{:S(2)}) copy-start(f32[512,1536]{1,0:T(8,128)} %copy-done.1) | copy-start | bytes 9437188
  119.5 3.5 %copy-start.4 = (bf16[512,1024]{1,0:T(8,128)(2,1)S(1)}, bf16[512,1024]{1,0:T(8,128)(2,1)}, u32[]{:S(2)}) copy-start(bf16[512,1024]{1,0:T(8,128)(2,1)} %param.10) | copy-start | bytes 3145732
  130.4 19.8 %slice-start = ((f32[32,2688]{1,0:T(8,128)}), f32[32,1536]{1,0:T(8,128)S(1)}, s32[]{:S(2)}) async-start(f32[32,2688]{1,0:T(8,128)} %copy-done.5), calls=%async_computation.3 | async-start | bytes 393216 | tf_op jit(solution)/shard_map/slice | solution.py:65
  130.4 157.2 %all-to-all-start = ((bf16[16,64,3072]{2,1,0:T(8,128)(2,1)}), bf16[16,64,3072]{2,1,0:T(8,128)(2,1)}, u32[]{:S(2)}, u32[]{:S(2)}) async-start(bf16[16,64,3072]{2,1,0:T(8,128)(2,1)} %pad_maximum_fusion), calls=%async_computation.1 | async-start | bytes 12582912 | tf_op jit(solution)/shard_map/all_to_all | solution.py:107
Sparse Core Ops, SparseCore 0:
  11.6 54.5 reduce-scatter.1
where the time goes:
time: 301 us
  waiting for transfers between devices  157 us (52%)
  blocking collectives  63.7 us (21%)
  matrix products  25.1 us (8%)
  starting transfers between devices  19.8 us (7%)
  between operations  16.8 us (6%)
  other arithmetic  15.9 us (5%)
    all_to_all x1, waiting for transfers between devices, per_device(): lax.all_to_all(terms.reshape(dp, rows, 2 * hidden_width), 'dp', 0, 0)  136 us
    psum x1, blocking collectives, per_device(): gram_raw = lax.psum(gram_part, 'dp')  45.7 us
    reduce_scatter x1, waiting for transfers between devices, per_device(): lax.psum_scatter(partial_attn, 'dp', scatter_dimension=1, tiled=True)  20.7 us
    all_to_all x1, starting transfers between devices, per_device(): lax.all_to_all(terms.reshape(dp, rows, 2 * hidden_width), 'dp', 0, 0)  19.8 us
    all_gather x1, blocking collectives, per_device(): packed_all = lax.all_gather(packed, 'dp', axis=0, tiled=True)  18 us
  transfers between devices with their start and end apart: 2, of which 2 were waited for; matrix products, arithmetic and copies ran while one was open for 6% of the time, Pallas kernels for 0%

commit v1 on v0

--- a/solution.py
+++ b/solution.py
@@ -61,7 +61,16 @@
     packed = jnp.concatenate(
         [hidden_sum, state_sum, jnp.broadcast_to(counts[:, None], (doc_dev, 128))], axis=1
     )
-    packed_all = lax.all_gather(packed, "dp", axis=0, tiled=True)
+    ways = lax.axis_size("dp")
+    up = [(d, (d + 1) % ways) for d in range(ways)]
+    down = [(d, (d - 1) % ways) for d in range(ways)]
+    earlier, later = ([packed], [packed])
+    for _ in range(ways // 2):
+        earlier.append(lax.ppermute(earlier[-1], "dp", up))
+    for _ in range((ways - 1) // 2):
+        later.append(lax.ppermute(later[-1], "dp", down))
+    line = jnp.concatenate([*earlier[::-1], *later[1:]], axis=0)
+    packed_all = jnp.roll(line, (lax.axis_index("dp") - ways // 2) * packed.shape[0], axis=0)
     hidden_all = packed_all[:, :hidden_width]
     state_all = packed_all[:, hidden_width : hidden_width + model_width]
     count_all = packed_all[:, hidden_width + model_width :][:, :1]

time: 301 us -> 312 us (1.037)
  starting transfers between devices: 19.8 us -> 40.8 us
  blocking collectives: 63.7 us -> 45.7 us
  local copies, waits for them, and re-layouts: 2.4 us -> 7.56 us
    ppermute x0 -> x15, starting transfers between devices: none -> 21.1 us  [the longest x8 21.1 us: per_device(): earlier.append(lax.ppermute(earlier[-1], 'dp', up))]
    all_gather x1 -> x0, blocking collectives: 18 us -> none  [per_device(): packed_all = lax.all_gather(packed, 'dp', axis=0, tiled=True)]
    ppermute x0 -> x15, waiting for transfers between devices: none -> 8.43 us  [the longest x7 8.41 us: per_device(): later.append(lax.ppermute(later[-1], 'dp', down))]
    reduce_scatter x1, waiting for transfers between devices: 20.7 us -> 14 us  [per_device(): lax.psum_scatter(partial_attn, 'dp', scatter_dimension=1, tiled=True)]
    concatenate x0 -> x1, local copies, waits for them, and re-layouts: none -> 5.6 us  [per_device(): jnp.roll(line, (lax.axis_index('dp') - ways // 2) * packed.shape[0], axis=0)]
  transfers between devices with their start and end apart: 2 -> 17, of which waited for: 2 -> 9; matrix products, arithmetic and copies ran while one was open for 6% -> 5% of each run, Pallas kernels for 0% -> 0%
where the time goes in v1:
time: 312 us
  waiting for transfers between devices  158 us (51%)
  blocking collectives  45.7 us (15%)
  starting transfers between devices  40.8 us (13%)
  matrix products  24.2 us (8%)
  other arithmetic  18.6 us (6%)
  between operations  16.8 us (5%)
  local copies, waits for them, and re-layouts  7.56 us (2%)
    all_to_all x1, waiting for transfers between devices, per_device(): lax.all_to_all(terms.reshape(dp, rows, 2 * hidden_width), 'dp', 0, 0)  135 us
    psum x1, blocking collectives, per_device(): gram_raw = lax.psum(gram_part, 'dp')  45.7 us
    ppermute x8, starting transfers between devices, per_device(): earlier.append(lax.ppermute(earlier[-1], 'dp', up))  21.1 us
    all_to_all x1, starting transfers between devices, per_device(): lax.all_to_all(terms.reshape(dp, rows, 2 * hidden_width), 'dp', 0, 0)  19.6 us
    reduce_scatter x1, waiting for transfers between devices, per_device(): lax.psum_scatter(partial_attn, 'dp', scatter_dimension=1, tiled=True)  14 us
    ppermute x7, waiting for transfers between devices, per_device(): later.append(lax.ppermute(later[-1], 'dp', down))  8.41 us
  transfers between devices with their start and end apart: 17, of which 9 were waited for; matrix products, arithmetic and copies ran while one was open for 5% of the time, Pallas kernels for 0%

profile of v1, /device:TPU:13, one launch (start us, length us, event | category | flops | bytes accessed | tf_op | source)
XLA Modules:
  0.0 311.6 jit_solution(5304353364659705585)
XLA Ops:
  7.2 0.0 copy-start
  7.2 0.0 reduce-scatter.2.cloned.1.call-start
  7.2 0.8 convert_element_type.61
  8.0 0.8 fusion.34
  8.9 1.5 multiply_reduce_fusion.1
  10.4 0.7 convert_element_type.57
  11.1 1.5 multiply_reduce_fusion
  12.6 0.0 copy-start.3
  12.6 4.2 %fusion.36 = f32[512,1536]{1,0:T(8,128)S(1)} fusion(bf16[1024,1536]{1,0:T(8,128)(2,1)} %param.13, f32[1024]{0:T(1024)S(1)} %convert_element_type.57, f32[512]{0:T(512)S(1)} %add_rsqrt_fusion, bf16[512,1024]{1,0:T(8,128)(2,1)} %param.10), kind=kOutput, calls=%fused_computation.64 | convolution fusion | flops 1612709888 | bytes 7346176 | tf_op jit(solution)/shard_map/dot_general | solution.py:48
  16.8 0.0 copy-start.5
  16.8 0.0 copy-start.6
  16.8 3.9 %fusion = (f32[2,1536]{1,0:T(2,128)S(1)}, f32[512,1536]{1,0:T(8,128)}) fusion(f32[2,256]{1,0:T(2,128)S(1)} %get-tuple-element.11, f32[512,1536]{1,0:T(8,128)S(1)} %fusion.36, bf16[1024,1536]{1,0:T(8,128)(2,1)S(1)} %copy-done, f32[1024]{0:T(1024)S(1)} %convert_element_type.57, f32[512]{0:T(512)S(1)} %add_rsqrt_fusion, bf16[512,1024]{1,0:T(8,128)(2,1)S(1)} %copy-done.3), kind=kOutput, calls=%fused_computation.5 | convolution fusion | flops 1619784704 | bytes 10506240 | tf_op jit(solution)/shard_map/dot_general | solution.py:49
  20.7 0.1 broadcast_in_dim.2
  20.8 1.9 collective-permute-start
  22.7 1.3 fusion.38
  23.9 0.0 reduce-scatter.2.cloned.1.call-update
  24.0 0.1 collective-permute-start.8
  24.0 0.0 collective-permute-done
  24.0 2.7 collective-permute-start.1
  26.8 1.4 collective-permute-done.8
  28.1 0.0 collective-permute-start.9
  28.1 0.0 collective-permute-done.1
  28.1 2.7 collective-permute-start.2
  30.9 1.4 collective-permute-done.9
  32.3 0.0 collective-permute-start.10
  32.3 0.0 collective-permute-done.2
  32.3 2.7 collective-permute-start.3
  35.0 1.4 collective-permute-done.10
  36.4 0.0 collective-permute-start.11
  36.4 0.0 collective-permute-done.3
  36.4 2.7 collective-permute-start.4
  39.1 1.4 collective-permute-done.11
  40.5 0.0 collective-permute-start.12
  40.5 0.0 collective-permute-done.4
  40.5 2.7 collective-permute-start.5
  43.2 1.4 collective-permute-done.12
  44.6 2.7 collective-permute-start.6
  47.4 1.4 collective-permute-done.13
  48.7 0.0 collective-permute-start.14
  48.7 2.7 collective-permute-start.7
  51.5 1.3 dynamic-slice_convert_fusion
  52.8 0.2 collective-permute-done.14
  53.0 0.0 collective-permute-done.7
  53.0 5.6 %concatenate.19 = f32[64,2688]{1,0:T(8,128)} concatenate(f32[2,2688]{1,0:T(2,128)S(1)} %collective-permute-done.7, f32[2,2688]{1,0:T(2,128)S(1)} %collective-permute-done.6, f32[2,2688]{1,0:T(2,128)S(1)} %collective-permute-done.5, f32[2,2688]{1,0:T(2,128)S(1)} %collective-permute-done.4, f32[2,2688]{1,0:T(2,128)S(1)} %collective-permute-done.3, ...), dimensions={0} | concatenate | bytes 1376256 | tf_op jit(solution)/shard_map/jit(_roll_dynamic)/concatenate | solution.py:73
  58.6 0.9 dynamic-slice_reduce_fusion
  59.5 3.8 %multiply_reduce_fusion.3 = (f32[32]{0:T(128)S(1)}, f32[32,1024]{1,0:T(8,128)S(1)}) fusion(f32[32]{0:T(128)S(1)} %dynamic-slice_reduce_fusion, bf16[1536,1024]{1,0:T(8,128)(2,1)} %param.15, f32[64,2688]{1,0:T(8,128)} %concatenate.19, s32[]{:T(128)S(6)} %select_n.24, s32[]{:T(128)S(6)} %add.95), kind=kOutput, calls=%fused_computation.27 | convolution fusion | flops 604110848 | bytes 3606272 | tf_op jit(solution)/shard_map/dot_general | solution.py:84
  63.4 14.0 %reduce-scatter.2.cloned.1.call-done = f32[32,256]{1,0:T(8,128)} async-done(((f32[32,4096]{1,0:T(8,128)}), f32[32,256]{1,0:T(8,128)}) %reduce-scatter.2.cloned.1.call-update) | async-done | bytes 32784 | tf_op jit(solution)/shard_map/reduce_scatter | solution.py:40
  77.4 1.0 fusion.11
  78.4 45.7 %psum.7 = f32[32,32]{1,0:T(8,128)S(1)} all-reduce(f32[32,32]{1,0:T(8,128)S(1)} %fusion.11), channel_id=1, replica_groups=mesh['groups'=2,'dp'=16] {'dp'}, use_global_device_ids=true, to_apply=%region_5.6 | all-reduce | flops 1024 | bytes 8192 | tf_op jit(solution)/shard_map/psum | solution.py:77
  124.1 0.1 fusion.23
  124.2 0.7 multiply_reduce_fusion.4
  125.6 0.8 multiply_reduce_fusion.5
  127.1 0.4 multiply_reduce_fusion.2
  127.5 0.1 divide_convert_fusion
  127.6 3.1 fusion.26
  130.7 3.5 %fusion.5 = (bf16[512,1536]{1,0:T(8,128)(2,1)S(1)}, bf16[512,1536]{1,0:T(8,128)(2,1)S(1)}) fusion(f32[512,1536]{1,0:T(8,128)} %get-tuple-element.13, f32[512,1536]{1,0:T(8,128)S(1)} %copy-done.2, f32[512]{0:T(512)S(1)} %bitcast.36, f32[2,1536]{1,0:T(2,128)S(1)} %fusion.26), kind=kLoop, calls=%fused_computation.11 | loop fusion | flops 11010048 | bytes 9451520 | tf_op jit(solution)/shard_map/convert_element_type | solution.py:111
  134.2 1.9 convolution_convert_fusion.1
  136.2 1.9 convolution_convert_fusion
  138.1 3.5 %pad_maximum_fusion = bf16[16,64,3072]{2,1,0:T(8,128)(2,1)} fusion(bf16[16,64,1536]{2,1,0:T(8,128)(2,1)S(1)} %bitcast.35, bf16[16,64,1536]{2,1,0:T(8,128)(2,1)S(1)} %bitcast.34), kind=kLoop, calls=%fused_computation.1 | loop fusion | flops 12582912 | bytes 12582912 | tf_op jit(solution)/shard_map/concatenate | solution.py:114
  141.6 19.6 %all-to-all-start = ((bf16[16,64,3072]{2,1,0:T(8,128)(2,1)}), bf16[16,64,3072]{2,1,0:T(8,128)(2,1)}, u32[]{:S(2)}, u32[]{:S(2)}) async-start(bf16[16,64,3072]{2,1,0:T(8,128)(2,1)} %pad_maximum_fusion), calls=%async_computation.1 | async-start | bytes 12582912 | tf_op jit(solution)/shard_map/all_to_all | solution.py:116
  161.3 2.0 fusion.15
  163.2 135.4 %all-to-all-done = bf16[16,64,3072]{2,1,0:T(8,128)(2,1)} async-done(((bf16[16,64,3072]{2,1,0:T(8,128)(2,1)}), bf16[16,64,3072]{2,1,0:T(8,128)(2,1)}, u32[]{:S(2)}, u32[]{:S(2)}) %all-to-all-start) | async-done | bytes 6291488 | tf_op jit(solution)/shard_map/all_to_all | solution.py:116
  298.6 4.0 %convert_reduce_fusion = f32[64,3072]{1,0:T(8,128)S(1)} fusion(bf16[16,64,3072]{2,1,0:T(8,128)(2,1)} %all-to-all-done), kind=kLoop, calls=%fused_computation | loop fusion | flops 6094848 | bytes 7077888 | tf_op jit(solution)/shard_map/reduce_sum | solution.py:117
  302.7 0.9 fusion.37
  (20 shorter events, 0.1 us)
Async XLA Ops:
  7.2 9.6 %copy-start = (bf16[1024,1536]{1,0:T(8,128)(2,1)S(1)}, bf16[1024,1536]{1,0:T(8,128)(2,1)}, u32[]{:S(2)}) copy-start(bf16[1024,1536]{1,0:T(8,128)(2,1)} %param.14) | copy-start | bytes 9437188
  7.2 70.2 %reduce-scatter.2.cloned.1.call-start = ((), (), s32[]{:S(2)}) async-start(), calls=%async_computation.2 | async-start | bytes 557056 | tf_op jit(solution)/shard_map/reduce_scatter | solution.py:40
  12.6 4.2 %copy-start.3 = (bf16[512,1024]{1,0:T(8,128)(2,1)S(1)}, bf16[512,1024]{1,0:T(8,128)(2,1)}, u32[]{:S(2)}) copy-start(bf16[512,1024]{1,0:T(8,128)(2,1)} %param.10) | copy-start | bytes 3145732
  16.8 3.9 %copy-start.1 = (f32[512,1536]{1,0:T(8,128)}, f32[512,1536]{1,0:T(8,128)S(1)}, u32[]{:S(2)}) copy-start(f32[512,1536]{1,0:T(8,128)S(1)} %fusion.36) | copy-start | bytes 9437188
  16.8 5.8 %copy-start.5 = (bf16[256,4096]{1,0:T(8,128)(2,1)S(1)}, bf16[256,4096]{1,0:T(8,128)(2,1)}, u32[]{:S(2)}) copy-start(bf16[256,4096]{1,0:T(8,128)(2,1)} %param.17) | copy-start | bytes 6291460
  16.8 5.8 %copy-start.6 = (bf16[32,256]{1,0:T(8,128)(2,1)S(1)}, bf16[32,256]{1,0:T(8,128)(2,1)}, u32[]{:S(2)}) copy-start(bf16[32,256]{1,0:T(8,128)(2,1)} %param.16) | copy-start | bytes 49156
  20.8 3.2 %collective-permute-start = (f32[2,2688]{1,0:T(2,128)S(1)}, f32[2,2688]{1,0:T(2,128)S(1)}, u32[]{:S(2)}, u32[]{:S(2)}) collective-permute-start(f32[2,2688]{1,0:T(2,128)S(1)} %pad_maximum_fusion.1), channel_id=1, source_target_pairs={{0,1},{1,2},{2,3},{3,4},{4,5},{5,6},{6,7},{7,8},{8,9},{9,10},{10,1... | collective-permute-start | bytes 64520 | tf_op jit(solution)/shard_map/ppermute | solution.py:69
  24.0 4.2 %collective-permute-start.8 = (f32[2,2688]{1,0:T(2,128)S(1)}, f32[2,2688]{1,0:T(2,128)S(1)}, u32[]{:S(2)}, u32[]{:S(2)}) collective-permute-start(f32[2,2688]{1,0:T(2,128)S(1)} %pad_maximum_fusion.1), channel_id=1, source_target_pairs={{0,15},{1,0},{2,1},{3,2},{4,3},{5,4},{6,5},{7,6},{8,7},{9,8},{10,9... | collective-permute-start | bytes 64520 | tf_op jit(solution)/shard_map/ppermute | solution.py:71
  24.0 4.1 %collective-permute-start.1 = (f32[2,2688]{1,0:T(2,128)S(1)}, f32[2,2688]{1,0:T(2,128)S(1)}, u32[]{:S(2)}, u32[]{:S(2)}) collective-permute-start(f32[2,2688]{1,0:T(2,128)S(1)} %collective-permute-done), channel_id=1, source_target_pairs={{0,1},{1,2},{2,3},{3,4},{4,5},{5,6},{6,7},{7,8},{8,9},{9,10},{10,1... | collective-permute-start | bytes 64520 | tf_op jit(solution)/shard_map/ppermute | solution.py:69
  28.1 4.1 %collective-permute-start.9 = (f32[2,2688]{1,0:T(2,128)S(1)}, f32[2,2688]{1,0:T(2,128)S(1)}, u32[]{:S(2)}, u32[]{:S(2)}) collective-permute-start(f32[2,2688]{1,0:T(2,128)S(1)} %collective-permute-done.8), channel_id=1, source_target_pairs={{0,15},{1,0},{2,1},{3,2},{4,3},{5,4},{6,5},{7,6},{8,7},{9,8},{10,9... | collective-permute-start | bytes 64520 | tf_op jit(solution)/shard_map/ppermute | solution.py:71
  28.1 4.1 %collective-permute-start.2 = (f32[2,2688]{1,0:T(2,128)S(1)}, f32[2,2688]{1,0:T(2,128)S(1)}, u32[]{:S(2)}, u32[]{:S(2)}) collective-permute-start(f32[2,2688]{1,0:T(2,128)S(1)} %collective-permute-done.1), channel_id=1, source_target_pairs={{0,1},{1,2},{2,3},{3,4},{4,5},{5,6},{6,7},{7,8},{8,9},{9,10},{10,1... | collective-permute-start | bytes 64520 | tf_op jit(solution)/shard_map/ppermute | solution.py:69
  32.3 4.1 %collective-permute-start.10 = (f32[2,2688]{1,0:T(2,128)S(1)}, f32[2,2688]{1,0:T(2,128)S(1)}, u32[]{:S(2)}, u32[]{:S(2)}) collective-permute-start(f32[2,2688]{1,0:T(2,128)S(1)} %collective-permute-done.9), channel_id=1, source_target_pairs={{0,15},{1,0},{2,1},{3,2},{4,3},{5,4},{6,5},{7,6},{8,7},{9,8},{10,9... | collective-permute-start | bytes 64520 | tf_op jit(solution)/shard_map/ppermute | solution.py:71
  32.3 4.1 %collective-permute-start.3 = (f32[2,2688]{1,0:T(2,128)S(1)}, f32[2,2688]{1,0:T(2,128)S(1)}, u32[]{:S(2)}, u32[]{:S(2)}) collective-permute-start(f32[2,2688]{1,0:T(2,128)S(1)} %collective-permute-done.2), channel_id=1, source_target_pairs={{0,1},{1,2},{2,3},{3,4},{4,5},{5,6},{6,7},{7,8},{8,9},{9,10},{10,1... | collective-permute-start | bytes 64520 | tf_op jit(solution)/shard_map/ppermute | solution.py:69
  36.4 4.1 %collective-permute-start.11 = (f32[2,2688]{1,0:T(2,128)S(1)}, f32[2,2688]{1,0:T(2,128)S(1)}, u32[]{:S(2)}, u32[]{:S(2)}) collective-permute-start(f32[2,2688]{1,0:T(2,128)S(1)} %collective-permute-done.10), channel_id=1, source_target_pairs={{0,15},{1,0},{2,1},{3,2},{4,3},{5,4},{6,5},{7,6},{8,7},{9,8},{10,9... | collective-permute-start | bytes 64520 | tf_op jit(solution)/shard_map/ppermute | solution.py:71
  36.4 4.1 %collective-permute-start.4 = (f32[2,2688]{1,0:T(2,128)S(1)}, f32[2,2688]{1,0:T(2,128)S(1)}, u32[]{:S(2)}, u32[]{:S(2)}) collective-permute-start(f32[2,2688]{1,0:T(2,128)S(1)} %collective-permute-done.3), channel_id=1, source_target_pairs={{0,1},{1,2},{2,3},{3,4},{4,5},{5,6},{6,7},{7,8},{8,9},{9,10},{10,1... | collective-permute-start | bytes 64520 | tf_op jit(solution)/shard_map/ppermute | solution.py:69
  40.5 4.1 %collective-permute-start.12 = (f32[2,2688]{1,0:T(2,128)S(1)}, f32[2,2688]{1,0:T(2,128)S(1)}, u32[]{:S(2)}, u32[]{:S(2)}) collective-permute-start(f32[2,2688]{1,0:T(2,128)S(1)} %collective-permute-done.11), channel_id=1, source_target_pairs={{0,15},{1,0},{2,1},{3,2},{4,3},{5,4},{6,5},{7,6},{8,7},{9,8},{10,9... | collective-permute-start | bytes 64520 | tf_op jit(solution)/shard_map/ppermute | solution.py:71
  40.5 4.1 %collective-permute-start.5 = (f32[2,2688]{1,0:T(2,128)S(1)}, f32[2,2688]{1,0:T(2,128)S(1)}, u32[]{:S(2)}, u32[]{:S(2)}) collective-permute-start(f32[2,2688]{1,0:T(2,128)S(1)} %collective-permute-done.4), channel_id=1, source_target_pairs={{0,1},{1,2},{2,3},{3,4},{4,5},{5,6},{6,7},{7,8},{8,9},{9,10},{10,1... | collective-permute-start | bytes 64520 | tf_op jit(solution)/shard_map/ppermute | solution.py:69
  44.6 4.1 %collective-permute-start.13 = (f32[2,2688]{1,0:T(2,128)S(1)}, f32[2,2688]{1,0:T(2,128)S(1)}, u32[]{:S(2)}, u32[]{:S(2)}) collective-permute-start(f32[2,2688]{1,0:T(2,128)S(1)} %collective-permute-done.12), channel_id=1, source_target_pairs={{0,15},{1,0},{2,1},{3,2},{4,3},{5,4},{6,5},{7,6},{8,7},{9,8},{10,9... | collective-permute-start | bytes 64520 | tf_op jit(solution)/shard_map/ppermute | solution.py:71
  44.6 4.1 %collective-permute-start.6 = (f32[2,2688]{1,0:T(2,128)S(1)}, f32[2,2688]{1,0:T(2,128)S(1)}, u32[]{:S(2)}, u32[]{:S(2)}) collective-permute-start(f32[2,2688]{1,0:T(2,128)S(1)} %collective-permute-done.5), channel_id=1, source_target_pairs={{0,1},{1,2},{2,3},{3,4},{4,5},{5,6},{6,7},{7,8},{8,9},{9,10},{10,1... | collective-permute-start | bytes 64520 | tf_op jit(solution)/shard_map/ppermute | solution.py:69
  48.7 4.3 %collective-permute-start.14 = (f32[2,2688]{1,0:T(2,128)S(1)}, f32[2,2688]{1,0:T(2,128)S(1)}, u32[]{:S(2)}, u32[]{:S(2)}) collective-permute-start(f32[2,2688]{1,0:T(2,128)S(1)} %collective-permute-done.13), channel_id=1, source_target_pairs={{0,15},{1,0},{2,1},{3,2},{4,3},{5,4},{6,5},{7,6},{8,7},{9,8},{10,9... | collective-permute-start | bytes 64520 | tf_op jit(solution)/shard_map/ppermute | solution.py:71
  48.7 4.3 %collective-permute-start.7 = (f32[2,2688]{1,0:T(2,128)S(1)}, f32[2,2688]{1,0:T(2,128)S(1)}, u32[]{:S(2)}, u32[]{:S(2)}) collective-permute-start(f32[2,2688]{1,0:T(2,128)S(1)} %collective-permute-done.6), channel_id=1, source_target_pairs={{0,1},{1,2},{2,3},{3,4},{4,5},{5,6},{6,7},{7,8},{8,9},{9,10},{10,1... | collective-permute-start | bytes 64520 | tf_op jit(solution)/shard_map/ppermute | solution.py:69
  58.6 18.8 %copy-start.7 = (f32[256]{0:T(256)S(1)}, f32[256]{0:T(256)}, u32[]{:S(2)}) copy-start(f32[256]{0:T(256)} %dynamic-slice_convert_fusion) | copy-start | bytes 3076
  127.1 3.5 %copy-start.2 = (f32[512,1536]{1,0:T(8,128)S(1)}, f32[512,1536]{1,0:T(8,128)}, u32[]{:S(2)}) copy-start(f32[512,1536]{1,0:T(8,128)} %copy-done.1) | copy-start | bytes 9437188
  130.7 3.5 %copy-start.4 = (bf16[512,1024]{1,0:T(8,128)(2,1)S(1)}, bf16[512,1024]{1,0:T(8,128)(2,1)}, u32[]{:S(2)}) copy-start(bf16[512,1024]{1,0:T(8,128)(2,1)} %param.10) | copy-start | bytes 3145732
  141.6 157.1 %all-to-all-start = ((bf16[16,64,3072]{2,1,0:T(8,128)(2,1)}), bf16[16,64,3072]{2,1,0:T(8,128)(2,1)}, u32[]{:S(2)}, u32[]{:S(2)}) async-start(bf16[16,64,3072]{2,1,0:T(8,128)(2,1)} %pad_maximum_fusion), calls=%async_computation.1 | async-start | bytes 12582912 | tf_op jit(solution)/shard_map/all_to_all | solution.py:116
Sparse Core Ops, SparseCore 0:
  24.1 53.2 reduce-scatter.1
